TPU v7x, 128 devices: a whole 4x4x4 slice. The times are simulated.
128 devices in a mesh: dp: 32 (over z, x, core), section: 4 (over y).
Axes of the slice: x: 4, y: 4, z: 4, core: 2. Of those that a mesh axis runs over, the one named last changes fastest.
Arguments:
- pair_grads: float32 [32, 4, 2, 1024, 256], P('dp', 'section'), may hold values from -80 to 80
- value_grads: float32 [32, 4, 1024, 1024], P('dp', 'section'), may hold values from -80 to 80
- pair_errors: float32 [32, 4, 2, 1024, 256], P('dp', 'section'), may hold values from -6 to 6
- value_errors: float32 [32, 4, 1024, 1024], P('dp', 'section'), may hold values from -6 to 6
- pair_basis: float32 [4, 2, 32, 256], P('section'), may hold values from -6 to 6
- value_basis: float32 [4, 32, 1024], P('section'), may hold values from -6 to 6
- pair_moment: float32 [4, 2, 1024, 256], P('section', None, 'dp'), may hold values from -6 to 6
- value_moment: float32 [4, 1024, 1024], P('section', 'dp'), may hold values from -6 to 6
- pair_weights: float32 [4, 2, 1024, 256], P('section', None, 'dp'), may hold values from -0.1875 to 0.1875
- value_weights: float32 [4, 1024, 1024], P('section', 'dp'), may hold values from -0.1875 to 0.1875
- gain_grads: float32 [32, 4, 2, 1024], P('dp', 'section'), may hold values from -6 to 6
- norm_gains: float32 [4, 2, 1024], P('section'), may hold values from 0.5 to 1.5
Outputs:
- pair_params: float32 [4, 2, 1024, 256], P('section', None, 'dp')
- value_params: float32 [4, 1024, 1024], P('section', 'dp')
- pair_velocity: float32 [4, 2, 1024, 256], P('section', None, 'dp')
- value_velocity: float32 [4, 1024, 1024], P('section', 'dp')
- gain_params: float32 [4, 2, 1024], P('section')
- pair_residue: float32 [32, 4, 2, 1024, 256], P('dp', 'section')
- value_residue: float32 [32, 4, 1024, 1024], P('dp', 'section')
- pair_factor: float32 [4, 2, 32, 256], P('section')
- value_factor: float32 [4, 32, 1024], P('section')
All inputs are finite; a program needn't handle non-finite values.
Results may differ from a plain program's by a relative error of at most 0.00012.
Values sent between devices are 32-bit elements; how exact they have to be, the bound alone decides.
A program may use at most 128 MiB of HBM per device.

v0:
```python
import jax
import jax.numpy as jnp
from jax import lax
from jax.sharding import PartitionSpec as P

ROUNDS = 2


highest = lax.Precision.HIGHEST
momentum_rate = 0.9
step_rate = 0.3


def whiten(gram, factor):
    lower = jnp.linalg.cholesky(gram)
    return lax.linalg.triangular_solve(lower, factor, left_side=True, lower=True)


def gram_of(factor):
    return jnp.einsum("...rk,...sk->...rs", factor, factor, precision=highest)


def orthonormal(factor):
    return whiten(gram_of(factor), factor)


def local(
    pair_grads,
    value_grads,
    pair_errors,
    value_errors,
    pair_basis,
    value_basis,
    pair_moment,
    value_moment,
    pair_weights,
    value_weights,
    gain_grads,
    norm_gains,
):
    replicas = lax.axis_size("dp")
    sections = lax.axis_size("section")
    pair_full = (pair_grads + pair_errors)[0]
    value_full = (value_grads + value_errors)[0]
    gain_mean = lax.psum(gain_grads[0], "dp") / replicas
    pair_right = pair_basis
    value_right = value_basis
    pair_left = None
    value_left = None
    for step in range(ROUNDS):
        pair_hat = orthonormal(pair_right)
        value_hat = orthonormal(value_right)
        pair_local = jnp.einsum("abrn,abmn->abrm", pair_hat, pair_full, precision=highest)
        value_local = jnp.einsum("arn,amn->arm", value_hat, value_full, precision=highest)
        pair_sum, value_sum = lax.psum((pair_local, value_local), "dp")
        pair_left = orthonormal(pair_sum)
        value_left = orthonormal(value_sum)
        pair_term = jnp.einsum("abrm,abmn->abrn", pair_left, pair_full, precision=highest)
        value_term = jnp.einsum("arm,amn->arn", value_left, value_full, precision=highest)
        pair_right, value_right = lax.psum((pair_term, value_term), "dp")
    pair_approx = jnp.einsum("abrm,abrn->abmn", pair_left, pair_right, precision=highest) / replicas
    value_approx = jnp.einsum("arm,arn->amn", value_left, value_right, precision=highest) / replicas
    pair_residue = (pair_full - pair_approx)[None]
    value_residue = (value_full - value_approx)[None]
    squares = jnp.sum(pair_approx * pair_approx) + jnp.sum(value_approx * value_approx)
    squares = squares + jnp.sum(gain_mean * gain_mean)
    total = lax.psum(squares, "section")
    layers_here = pair_full.shape[0]
    width = value_full.shape[1]
    narrow = pair_full.shape[3]
    entries = layers_here * sections * (2 * width * narrow + width * width + 2 * width)
    scale = 1.0 / jnp.sqrt(total / entries + 1e-06)
    rows_here = pair_moment.shape[2]
    start = lax.axis_index("dp") * rows_here
    pair_rows = lax.dynamic_slice_in_dim(pair_approx, start, rows_here, 2)
    value_rows = lax.dynamic_slice_in_dim(value_approx, start, rows_here, 1)
    pair_velocity = momentum_rate * pair_moment + scale * pair_rows
    value_velocity = momentum_rate * value_moment + scale * value_rows
    pair_params = pair_weights - step_rate * pair_velocity
    value_params = value_weights - step_rate * value_velocity
    gain_params = norm_gains - step_rate * scale * gain_mean
    return (
        pair_params,
        value_params,
        pair_velocity,
        value_velocity,
        gain_params,
        pair_residue,
        value_residue,
        pair_right,
        value_right,
    )


def solution(mesh):
    in_specs = (
        P("dp", "section", None, None, None),
        P("dp", "section", None, None),
        P("dp", "section", None, None, None),
        P("dp", "section", None, None),
        P("section", None, None, None),
        P("section", None, None),
        P("section", None, "dp", None),
        P("section", "dp", None),
        P("section", None, "dp", None),
        P("section", "dp", None),
        P("dp", "section", None, None),
        P("section", None, None),
    )
    out_specs = (
        P("section", None, "dp", None),
        P("section", "dp", None),
        P("section", None, "dp", None),
        P("section", "dp", None),
        P("section", None, None),
        P("dp", "section", None, None, None),
        P("dp", "section", None, None),
        P("section", None, None, None),
        P("section", None, None),
    )
    return jax.shard_map(local, mesh=mesh, in_specs=in_specs, out_specs=out_specs, check_vma=False)
```

profile of v0, /device:TPU:1, one launch (start us, length us, event | category | flops | bytes accessed | tf_op | source)
XLA Modules:
  0.0 577.5 jit_solution(8174329451514965076)
XLA Ops:
  8.5 5.9 %custom-call.26 = f32[1,2,32,32]{3,2,1,0:T(8,128)S(1)} custom-call(f32[1,2,32,32]{3,2,1,0:T(8,128)S(1)} %fusion.79), custom_call_target="Cholesky" | custom-call | tf_op jit(solution)/shard_map/jit(cholesky)/cholesky | solution.py:15
  14.6 4.9 custom-call.27
  21.0 2.9 custom-call.34
  36.8 4.6 fusion.24
  41.6 106.2 %all-reduce.15.cloned.1.call-done = (f32[1,2,32,1024]{3,2,1,0:T(8,128)}, f32[1,32,1024]{2,1,0:T(8,128)}) async-done(((f32[1,2,32,1024]{3,2,1,0:T(8,128)}, f32[1,32,1024]{2,1,0:T(8,128)}), (f32[1,2,32,1024]{3,2,1,0:T(8,128)}, f32[1,32,1024]{2,1,0:T(8,128)})) %all-reduce.15.cloned.1.call-update) | async-done | bytes 393232 | tf_op jit(solution)/shard_map/psum | solution.py:55
  149.3 5.9 %custom-call.28 = f32[1,2,32,32]{3,2,1,0:T(8,128)S(1)} custom-call(f32[1,2,32,32]{3,2,1,0:T(8,128)S(1)} %fusion.78), custom_call_target="Cholesky" | custom-call | tf_op jit(solution)/shard_map/jit(cholesky)/cholesky | solution.py:15
  155.4 4.9 custom-call.29
  165.0 2.9 custom-call.36
  172.9 5.3 fusion.27
  178.3 99.2 %all-reduce.13.cloned.1.call-done = (f32[1,2,32,256]{3,2,1,0:T(8,128)}, f32[1,32,1024]{2,1,0:T(8,128)}) async-done(((f32[1,2,32,256]{3,2,1,0:T(8,128)}, f32[1,32,1024]{2,1,0:T(8,128)}), (f32[1,2,32,256]{3,2,1,0:T(8,128)}, f32[1,32,1024]{2,1,0:T(8,128)})) %all-reduce.13.cloned.1.call-update) | async-done | bytes 196624 | tf_op jit(solution)/shard_map/psum | solution.py:60
  278.7 5.9 %custom-call.30 = f32[1,2,32,32]{3,2,1,0:T(8,128)S(1)} custom-call(f32[1,2,32,32]{3,2,1,0:T(8,128)S(1)} %fusion.77), custom_call_target="Cholesky" | custom-call | tf_op jit(solution)/shard_map/jit(cholesky)/cholesky | solution.py:15
  284.8 4.9 custom-call.31
  294.9 2.9 custom-call.38
  302.8 6.7 %fusion.30 = f32[1,32,1024]{2,1,0:T(8,128)} fusion(f32[32,1024]{1,0:T(8,128)S(1)} %fusion.55, f32[1,1,1024,1024]{3,2,1,0:T(8,128)} %copy-done.1), kind=kOutput, calls=%fused_computation.28 | convolution fusion | flops 402653184 | bytes 4456448 | tf_op jit(solution)/shard_map/arn,amn->arm/dot_general | solution.py:54
  309.6 64.3 %psum.78 = f32[1,2,1024]{2,1,0:T(2,128)S(1)} all-reduce(f32[1,2,1024]{2,1,0:T(2,128)S(1)} %bitcast.235), channel_id=1, replica_groups=mesh['dp'=32,'section'=4] {'dp'}, use_global_device_ids=true, to_apply=%region_14.20 | all-reduce | flops 2048 | bytes 16384 | tf_op jit(solution)/shard_map/psum | solution.py:45
  373.9 37.9 %all-reduce.11.cloned.1.call-done = (f32[1,2,32,1024]{3,2,1,0:T(8,128)}, f32[1,32,1024]{2,1,0:T(8,128)}) async-done(((f32[1,2,32,1024]{3,2,1,0:T(8,128)}, f32[1,32,1024]{2,1,0:T(8,128)}), (f32[1,2,32,1024]{3,2,1,0:T(8,128)}, f32[1,32,1024]{2,1,0:T(8,128)})) %all-reduce.11.cloned.1.call-update) | async-done | bytes 393232 | tf_op jit(solution)/shard_map/psum | solution.py:55
  413.2 6.1 %custom-call.32 = f32[1,2,32,32]{3,2,1,0:T(8,128)S(1)} custom-call(f32[1,2,32,32]{3,2,1,0:T(8,128)S(1)} %fusion.76), custom_call_target="Cholesky" | custom-call | tf_op jit(solution)/shard_map/jit(cholesky)/cholesky | solution.py:15
  419.5 4.9 custom-call.33
  429.1 2.9 custom-call.40
  437.0 5.3 fusion.33
  443.0 98.6 %all-reduce.9.cloned.1.call-done = (f32[1,2,32,256]{3,2,1,0:T(8,128)}, f32[1,32,1024]{2,1,0:T(8,128)}) async-done(((f32[1,2,32,256]{3,2,1,0:T(8,128)}, f32[1,32,1024]{2,1,0:T(8,128)}), (f32[1,2,32,256]{3,2,1,0:T(8,128)}, f32[1,32,1024]{2,1,0:T(8,128)})) %all-reduce.9.cloned.1.call-update) | async-done | bytes 196624 | tf_op jit(solution)/shard_map/psum | solution.py:60
  546.8 3.5 convolution_multiply_fusion
  550.4 3.9 fusion.8
  556.3 9.0 %psum.79 = f32[]{:T(128)} all-reduce(f32[]{:T(128)S(6)} %add.65), channel_id=1, replica_groups=mesh['dp'=32,'section'=4] {'section'}, use_global_device_ids=true, to_apply=%region_16.22 | all-reduce | flops 1 | bytes 8 | tf_op jit(solution)/shard_map/psum | solution.py:67
  (114 shorter events, 61.2 us)
Async XLA Ops:
  7.2 13.4 %copy-start = (f32[1,32,1024]{2,1,0:T(8,128)S(1)}, f32[1,32,1024]{2,1,0:T(8,128)}, u32[]{:S(2)}) copy-start(f32[1,32,1024]{2,1,0:T(8,128)} %param.25) | copy-start | bytes 393220
  7.2 140.6 %all-reduce.15.cloned.1.call-start = ((), (), s32[]{:S(2)}) async-start(), calls=%async_computation.3 | async-start | bytes 786432 | tf_op jit(solution)/shard_map/psum | solution.py:55
  28.0 5.4 copy-start.5
  28.0 5.4 copy-start.6
  34.8 2.0 copy-start.1
  41.4 236.1 %all-reduce.13.cloned.1.call-start = ((), (), s32[]{:S(2)}) async-start(), calls=%async_computation.2 | async-start | bytes 393216 | tf_op jit(solution)/shard_map/psum | solution.py:60
  178.3 233.5 %all-reduce.11.cloned.1.call-start = ((), (), s32[]{:S(2)}) async-start(), calls=%async_computation.1 | async-start | bytes 786432 | tf_op jit(solution)/shard_map/psum | solution.py:55
  277.5 32.1 %copy-start.14 = (f32[1,1,2,1024]{3,2,1,0:T(2,128)S(1)}, f32[1,1,2,1024]{3,2,1,0:T(2,128)}, u32[]{:S(2)}) copy-start(f32[1,1,2,1024]{3,2,1,0:T(2,128)} %param.30) | copy-start | bytes 24580
  309.5 232.1 %all-reduce.9.cloned.1.call-start = ((), (), s32[]{:S(2)}) async-start(), calls=%async_computation | async-start | bytes 393216 | tf_op jit(solution)/shard_map/psum | solution.py:60
  541.6 5.2 copy-start.7
  544.4 2.4 copy-start.4
  544.4 6.0 %copy-start.2 = (f32[1,1,1024,1024]{3,2,1,0:T(8,128)S(1)}, f32[1,1,1024,1024]{3,2,1,0:T(8,128)}, u32[]{:S(2)}) copy-start(f32[1,1,1024,1024]{3,2,1,0:T(8,128)} %copy-done.1) | copy-start | bytes 12582916
  550.3 4.0 copy-start.3
  550.3 15.6 %copy-start.11 = (f32[1,2,32,256]{3,2,1,0:T(8,128)S(1)}, f32[1,2,32,256]{3,2,1,0:T(8,128)}, u32[]{:S(2)}) copy-start(f32[1,2,32,256]{3,2,1,0:T(8,128)} %param.28) | copy-start | bytes 196612
  550.4 15.6 %copy-start.12 = (f32[1,2,32,256]{3,2,1,0:T(8,128)S(1)}, f32[1,2,32,256]{3,2,1,0:T(8,128)}, u32[]{:S(2)}) copy-start(f32[1,2,32,256]{3,2,1,0:T(8,128)} %param.26) | copy-start | bytes 196612
  550.4 17.1 %copy-start.9 = (f32[1,32,1024]{2,1,0:T(8,128)S(1)}, f32[1,32,1024]{2,1,0:T(8,128)}, u32[]{:S(2)}) copy-start(f32[1,32,1024]{2,1,0:T(8,128)} %param.29) | copy-start | bytes 393220
  550.4 17.1 %copy-start.10 = (f32[1,32,1024]{2,1,0:T(8,128)S(1)}, f32[1,32,1024]{2,1,0:T(8,128)}, u32[]{:S(2)}) copy-start(f32[1,32,1024]{2,1,0:T(8,128)} %param.27) | copy-start | bytes 393220
  550.4 18.7 %copy-start.13 = (f32[1,2,1024]{2,1,0:T(2,128)S(1)}, f32[1,2,1024]{2,1,0:T(2,128)}, u32[]{:S(2)}) copy-start(f32[1,2,1024]{2,1,0:T(2,128)} %param.31) | copy-start | bytes 24580
  550.4 19.3 %copy-start.8 = (f32[1,2,32,256]{3,2,1,0:T(8,128)S(1)}, f32[1,2,32,256]{3,2,1,0:T(8,128)}, u32[]{:S(2)}) copy-start(f32[1,2,32,256]{3,2,1,0:T(8,128)} %get-tuple-element.37) | copy-start | bytes 196612
Sparse Core Ops, SparseCore 0:
  41.5 106.2 all-reduce.14
  178.4 99.0 all-reduce.12
  309.6 102.0 all-reduce.10
  442.5 99.0 all-reduce.8
where the time goes:
time: 580 us; the launch traced here: 578 us
  waiting for transfers between devices  342 us (59%)
  other arithmetic  85.7 us (15%)
  blocking collectives  73.3 us (13%)
  matrix products  55.5 us (10%)
  between operations  16.8 us (3%)
    psum x2, waiting for transfers between devices, local(): pair_right, value_right = lax.psum((pair_term, value_term), 'dp')  198 us
    psum x2, waiting for transfers between devices, local(): pair_sum, value_sum = lax.psum((pair_local, value_local), 'dp')  144 us
    psum x1, blocking collectives, local(): gain_mean = lax.psum(gain_grads[0], 'dp') / replicas  64.3 us
    another operation x25, other arithmetic, whiten(): lower = jnp.linalg.cholesky(gram)  38.7 us
    another operation x17, other arithmetic, whiten(): lax.linalg.triangular_solve(lower, factor, left_side=True, lower=True)  32.3 us
  transfers between devices with their start and end apart: 4, of which 4 were waited for; matrix products, arithmetic and copies ran while one was open for 0% of the time, Pallas kernels for 0%

commit v1 on v0

v1 whole, which is shorter than its diff:
```python
import jax
import jax.numpy as jnp
from jax import lax
from jax.experimental import pallas as pl
from jax.experimental.pallas import tpu as pltpu
from jax.sharding import PartitionSpec as P

MESH = pl.DeviceIdType.MESH
f32, bf16 = jnp.float32, jnp.bfloat16
NN = (((1,), (0,)), ((), ()))
NT = (((1,), (1,)), ((), ()))
highest = lax.Precision.HIGHEST

D, QK, R = 1024, 256, 32
N_DP, SECTIONS = 32, 4
SIDE = 4
CHIPS = SIDE * SIDE
TILE = 128
momentum_rate = 0.9
step_rate = 0.3

OFFSETS = ((2, 2), (2, 1), (2, 3), (1, 2), (3, 2), (0, 2), (2, 0), (1, 1), (1, 3), (3, 1), (3, 3), (0, 1), (0, 3), (1, 0), (3, 0))

PRODUCT, BULK, GAIN_PAIR, GAIN_ALL, GAIN_MEAN, LEFT, RIGHT, TOTAL = range(8, 16)


def split(a):
    high = a.astype(bf16)
    return high, (a - high.astype(f32)).astype(bf16)


def gram(a):
    return lax.dot_general(a, a, NT, precision=highest, preferred_element_type=f32)


def whiten(inverse, a):
    return lax.dot_general(inverse, a, NN, precision=highest, preferred_element_type=f32)


def inverse_factors(grams):
    row = lax.broadcasted_iota(jnp.int32, (R, 2 * R), 0)
    col = lax.broadcasted_iota(jnp.int32, (R, 2 * R), 1)
    eye = (row[:, :R] == col[:, :R]).astype(f32)

    def step(k, carry):
        out = []
        for both, pivots in carry:
            pivot_row = jnp.sum(jnp.where(row == k, both, 0.0), axis=0, keepdims=True)
            column = jnp.sum(jnp.where(col == k, both, 0.0), axis=1, keepdims=True)
            pivot = jnp.sum(jnp.where(col[:1] == k, pivot_row, 0.0), axis=1, keepdims=True)
            pivots = jnp.where(row[:, :1] == k, pivot, pivots)
            times = jnp.where(row[:, :1] > k, column / pivot, 0.0)
            out.append((both - times * pivot_row, pivots))
        return tuple(out)

    start = tuple((jnp.concatenate([g, eye], axis=1), jnp.zeros((R, 1), f32)) for g in grams)
    done = lax.fori_loop(0, R, step, start)
    return [both[:, R:] / jnp.sqrt(pivots) for both, pivots in done]


def load_tiles(ref, first, tiles):
    return jnp.concatenate([ref[(first + t) * R : (first + t + 1) * R, :] for t in range(tiles)], axis=1)


def store_tiles(ref, first, value):
    for t in range(value.shape[1] // TILE):
        ref[(first + t) * R : (first + t + 1) * R, :] = value[:, t * TILE : (t + 1) * TILE]


def product(factor, high, low, dims):
    both = jnp.concatenate(split(factor), axis=0)
    out = lax.dot_general(both, high, dims, preferred_element_type=f32)
    out = out + lax.dot_general(both, low, dims, preferred_element_type=f32)
    return out[:R] + out[R:]


def kernel(
    pg, vg, pe, ve, pbasis, vbasis, pmoment, vmoment, pweights, vweights, ggrads, gnorm,
    pparams, vparams, pvel, vvel, gparams, presidue, vresidue, pfactor, vfactor,
    ep, ev, pb, vb, pm, vm, pw, vw, gg, gn,
    p_own, v_own, p_in, v_in, p_other, v_other, ph, plow, vh, vlow,
    v_pay, v_rs, v_res, pl_pay, pl_rs, pl_res, pr_pay, pr_rs, pr_res,
    g_own, g_pair, g_send, g_in, g_mean,
    lhv, lhp, rv, rp, ltv, ltp, part, totals,
    load, send, recv,
):
    d = lax.axis_index("dp")
    s = lax.axis_index("section")
    c = d % 2
    chip = d // 2
    z, x = chip // SIDE, chip % SIDE

    def chip_at(dz, dx):
        return ((z + dz) % SIDE) * SIDE + (x + dx) % SIDE

    partner = (chip * 2 + 1 - c, s)
    line = tuple((dy, dc) for dy in (2, 1, 3, 0) for dc in (0, 1) if dy or dc)

    def on_line(dy, dc):
        return (chip * 2 + (c + dc) % 2, (s + dy) % SECTIONS)

    loads = []

    def start_load(source, target):
        copy = pltpu.make_async_copy(source, target, load.at[len(loads)])
        loads.append(copy)
        return copy

    basis_loads = [start_load(pbasis, pb), start_load(vbasis, vb)]
    pair_loads = [
        (w, r, start_load(pg.at[w, pl.ds(r, 512)], presidue.at[w, pl.ds(r, 512)]), start_load(pe.at[w, pl.ds(r, 512)], ep.at[w, pl.ds(r, 512)]))
        for w in range(2)
        for r in range(0, D, 512)
    ]
    value_loads = [
        (r, start_load(vg.at[pl.ds(r, 256)], vresidue.at[pl.ds(r, 256)]), start_load(ve.at[pl.ds(r, 256)], ev.at[pl.ds(r, 256)]))
        for r in range(0, D, 256)
    ]
    gain_load = start_load(ggrads, gg)
    late_loads = [start_load(pmoment, pm), start_load(vmoment, vm), start_load(pweights, pw), start_load(vweights, vw), start_load(gnorm, gn)]

    for copy in basis_loads:
        copy.start()

    @pl.when(c == 0)
    def _():
        for _, _, a, b in pair_loads:
            a.start()
            b.start()
        for _, a, b in value_loads:
            a.start()
            b.start()

    @pl.when(c == 1)
    def _():
        for _, a, b in value_loads:
            a.start()
            b.start()
        for _, _, a, b in pair_loads:
            a.start()
            b.start()

    gain_load.start()
    for copy in late_loads:
        copy.start()

    barrier = pltpu.get_barrier_semaphore()
    for dz, dx in OFFSETS:
        pl.semaphore_signal(barrier, inc=1, device_id=(chip_at(dz, dx) * 2 + c, s), device_id_type=MESH)
    for dy, dc in line:
        pl.semaphore_signal(barrier, inc=1, device_id=on_line(dy, dc), device_id_type=MESH)

    def put(source, target, slot, device):
        pltpu.make_async_remote_copy(
            src_ref=source, dst_ref=target, send_sem=send.at[slot], recv_sem=recv.at[slot], device_id=device, device_id_type=MESH
        ).start()

    def arrived(ref, slot):
        pltpu.make_async_copy(ref, ref, recv.at[slot]).wait()

    def gone(ref, slot):
        pltpu.make_async_copy(ref, ref, send.at[slot]).wait()

    for copy in basis_loads:
        copy.wait()

    def pair_stage(out):
        for w, r, a, b in pair_loads:
            a.wait()
            b.wait()
            full = presidue[w, r : r + 512, :] + ep[w, r : r + 512, :]
            presidue[w, r : r + 512, :] = full
            store_tiles(out, w * 8 + r // TILE, product(pb[w], *split(full), NT))

    def value_stage(out):
        for r, a, b in value_loads:
            a.wait()
            b.wait()
            full = vresidue[r : r + 256, :] + ev[r : r + 256, :]
            vresidue[r : r + 256, :] = full
            store_tiles(out, r // TILE, product(vb[...], *split(full), NT))

    def spread_gain(core):
        gain_load.wait()
        for w in range(2):
            for t in range(8):
                g_own[w, t : t + 1, :] = gg[w : w + 1, t * TILE : (t + 1) * TILE]
        put(g_own.at[1 - core], g_pair, GAIN_PAIR, partner)

    def sum_over_plane(index, pay, rs, res, rows, first=None, second=None):
        slot = 2 * index
        for k, (dz, dx) in enumerate(OFFSETS):
            other = chip_at(dz, dx)
            put(pay.at[pl.ds(pl.multiple_of(other * rows, 8), rows)], rs.at[k], slot, (other * 2 + c, s))
        if first is not None:
            first()
        arrived(rs, slot)
        own = pl.ds(pl.multiple_of(chip * rows, 8), rows)
        total = pay[own, :]
        for k in range(CHIPS - 1):
            total = total + rs[k]
        res[own, :] = total
        for dz, dx in OFFSETS:
            put(res.at[own], res.at[own], slot + 1, (chip_at(dz, dx) * 2 + c, s))
        if second is not None:
            second()
        rest = res.at[pl.ds(0, (CHIPS - 1) * rows)]
        arrived(rest, slot + 1)
        gone(rs, slot)
        gone(rest, slot + 1)

    def transposed(factor, out):
        high, low = split(factor)
        high, low = high.astype(f32), low.astype(f32)
        out[...] = jnp.concatenate([high, high, low], axis=0).T.astype(bf16)

    def right_stack(right):
        high, low = split(right * (1.0 / N_DP))
        return jnp.concatenate([high, low, high], axis=0)

    def rounds(core, left_bufs, right_bufs, count, right_tiles, bases, mats):
        left_pay, left_rs, left_res, left_rows = left_bufs
        right_pay, right_rs, right_res, right_rows = right_bufs
        state = {}

        def lefts(ref):
            return [load_tiles(ref, w * 8, 8) for w in range(count)]

        def rights(ref):
            return [load_tiles(ref, w * right_tiles, right_tiles) for w in range(count)]

        def first_wait():
            state["inverse"] = inverse_factors([gram(b) for b in bases()])

        def gains():
            arrived(g_pair, GAIN_PAIR)
            gone(g_pair, GAIN_PAIR)
            g_send[...] = g_own[core] + g_pair[...]

        def chip_sums():
            if core == 0:
                arrived(v_other, BULK)
                gone(p_other, BULK)
                for r in range(0, D, 128):
                    vh[r : r + 128, :], vlow[r : r + 128, :] = split(vresidue[r : r + 128, :] + v_other[r : r + 128, :])
            else:
                arrived(p_other, BULK)
                gone(v_other, BULK)
                for w in range(2):
                    for r in range(0, D, 256):
                        ph[w, r : r + 256, :], plow[w, r : r + 256, :] = split(presidue[w, r : r + 256, :] + p_other[w, r : r + 256, :])
            gains()

        def spread_gains():
            for k, (dz, dx) in enumerate(OFFSETS):
                put(g_send, g_in.at[k], GAIN_ALL, (chip_at(dz, dx) * 2 + c, s))

        def gain_means():
            arrived(g_in, GAIN_ALL)
            gone(g_in, GAIN_ALL)
            total = g_send[...]
            for k in range(CHIPS - 1):
                total = total + g_in[k]
            g_mean[core] = total / N_DP
            put(g_mean.at[core], g_mean.at[core], GAIN_MEAN, partner)

        for step in range(2):
            last = step == 1
            sum_over_plane(2 * step, left_pay[step], left_rs[step], left_res[step], left_rows, state.pop("overlap", first_wait), None if last else chip_sums)
            if not last:
                spread_gains()
            left = [whiten(i, a) for i, a in zip(state["inverse"], lefts(left_res[step]))]
            for w, a in enumerate(left):
                store_tiles(right_pay[step], w * right_tiles, product(a, *mats(w), NN))

            def factor_left():
                state["inverse"] = inverse_factors([gram(a) for a in left])
                if last:
                    for w, (i, a) in enumerate(zip(state["inverse"], left)):
                        hat = whiten(i, a)
                        if core == 0:
                            lhv[...] = hat
                        else:
                            lhp[w] = hat

            def after():
                if last:
                    if core == 0:
                        put(lhv, lhv, LEFT, partner)
                        transposed(lhv[...], ltv)
                        arrived(lhp, LEFT)
                        gone(lhv, LEFT)
                        for w in range(2):
                            transposed(lhp[w], ltp.at[w])
                    else:
                        put(lhp, lhp, LEFT, partner)
                        for w in range(2):
                            transposed(lhp[w], ltp.at[w])
                        arrived(lhv, LEFT)
                        gone(lhp, LEFT)
                        transposed(lhv[...], ltv)
                else:
                    gain_means()

            sum_over_plane(2 * step + 1, right_pay[step], right_rs[step], right_res[step], right_rows, factor_left, after)
            right = [whiten(i, a) for i, a in zip(state["inverse"], rights(right_res[step]))]
            if not last:
                for w, a in enumerate(right):
                    store_tiles(left_pay[1], w * 8, product(a, *mats(w), NT))

                def factor_right():
                    state["inverse"] = inverse_factors([gram(a) for a in right])

                state["overlap"] = factor_right
        return right

    def value_approx():
        stack = right_stack(rv[...])
        for r in range(0, D, 256):
            term = lax.dot_general(ltv[r : r + 256, :], stack, NN, preferred_element_type=f32)
            vresidue[r : r + 256, :] = vresidue[r : r + 256, :] - term
        vfactor[...] = rv[...]

    def pair_approx():
        for w in range(2):
            stack = right_stack(rp[w])
            for r in range(0, D, 512):
                term = lax.dot_general(ltp[w, r : r + 512, :], stack, NN, preferred_element_type=f32)
                presidue[w, r : r + 512, :] = presidue[w, r : r + 512, :] - term
            pfactor[w] = rp[w]

    def squares(terms):
        total = jnp.zeros((8, TILE), f32)
        for term in terms:
            term = term * term
            for r in range(0, term.shape[0], 8):
                for t in range(0, term.shape[1], TILE):
                    total = total + term[r : r + 8, t : t + TILE]
        return total

    def send_part(core, rights):
        part[...] = squares(rights) / (N_DP * N_DP) + squares([g_mean[core]])
        for k, (dy, dc) in enumerate(line):
            put(part, totals.at[k], TOTAL, on_line(dy, dc))

    @pl.when(c == 0)
    def _():
        pair_stage(pl_pay.at[0])
        pl.semaphore_wait(barrier, len(OFFSETS) + len(line))
        put(pl_pay.at[0], p_in, PRODUCT, partner)
        spread_gain(0)
        value_stage(v_own)
        put(presidue, p_other, BULK, partner)
        arrived(v_in, PRODUCT)
        v_pay[0] = v_own[...] + v_in[...]
        gone(p_in, PRODUCT)
        bufs = [v_pay.at[0], v_pay.at[1]], [v_rs.at[0], v_rs.at[1]], [v_res.at[0], v_res.at[1]], 16
        more = [v_pay.at[2], v_pay.at[3]], [v_rs.at[2], v_rs.at[3]], [v_res.at[2], v_res.at[3]], 16
        (right,) = rounds(0, bufs, more, 1, 8, lambda: [vb[...]], lambda w: (vh[...], vlow[...]))
        rv[...] = right
        put(rv, rv, RIGHT, partner)
        send_part(0, [right])
        value_approx()
        arrived(rp, RIGHT)
        pair_approx()
        gone(rv, RIGHT)

    @pl.when(c == 1)
    def _():
        value_stage(v_own)
        pl.semaphore_wait(barrier, len(OFFSETS) + len(line))
        put(v_own, v_in, PRODUCT, partner)
        spread_gain(1)
        pair_stage(p_own)
        put(vresidue, v_other, BULK, partner)
        arrived(p_in, PRODUCT)
        pl_pay[0] = p_own[...] + p_in[...]
        gone(v_in, PRODUCT)
        bufs = [pl_pay.at[0], pl_pay.at[1]], [pl_rs.at[0], pl_rs.at[1]], [pl_res.at[0], pl_res.at[1]], 32
        more = [pr_pay.at[0], pr_pay.at[1]], [pr_rs.at[0], pr_rs.at[1]], [pr_res.at[0], pr_res.at[1]], 8
        right = rounds(1, bufs, more, 2, 2, lambda: [pb[0], pb[1]], lambda w: (ph[w], plow[w]))
        for w in range(2):
            rp[w] = right[w]
        put(rp, rp, RIGHT, partner)
        send_part(1, right)
        pair_approx()
        arrived(rv, RIGHT)
        value_approx()
        gone(rp, RIGHT)

    for copy in late_loads:
        copy.wait()
    arrived(totals, TOTAL)
    gone(totals, TOTAL)
    arrived(g_mean.at[0], GAIN_MEAN)
    gone(g_mean.at[0], GAIN_MEAN)
    total = part[...]
    for k in range(len(line)):
        total = total + totals[k]
    total = jnp.sum(jnp.sum(total, axis=0, keepdims=True), axis=1, keepdims=True)
    entries = SECTIONS * (2 * D * QK + D * D + 2 * D)
    scale = 1.0 / jnp.sqrt(total / entries + 1e-06)
    rows = pl.ds(pl.multiple_of(d * R, R), R)
    term = lax.dot_general(ltv[rows, :], right_stack(rv[...]), NN, preferred_element_type=f32)
    velocity = momentum_rate * vm[...] + scale * term
    vvel[...] = velocity
    vparams[...] = vw[...] - step_rate * velocity
    for w in range(2):
        term = lax.dot_general(ltp[w, rows, :], right_stack(rp[w]), NN, preferred_element_type=f32)
        velocity = momentum_rate * pm[w] + scale * term
        pvel[w] = velocity
        pparams[w] = pw[w] - step_rate * velocity
        for t in range(8):
            at = slice(t * TILE, (t + 1) * TILE)
            gparams[w : w + 1, at] = gn[w : w + 1, at] - step_rate * scale * g_mean[w, t : t + 1, :]


def local(
    pair_grads, value_grads, pair_errors, value_errors, pair_basis, value_basis,
    pair_moment, value_moment, pair_weights, value_weights, gain_grads, norm_gains,
):
    any_space = pl.BlockSpec(memory_space=pl.ANY)
    vmem = pl.BlockSpec(memory_space=pltpu.VMEM)

    def shape(*dims):
        return jax.ShapeDtypeStruct(dims, f32)

    def scratch(*dims, dtype=f32):
        return pltpu.VMEM(dims, dtype)

    out = pl.pallas_call(
        kernel,
        name="power_rounds",
        out_shape=(
            shape(2, R, QK), shape(R, D), shape(2, R, QK), shape(R, D), shape(2, D),
            shape(2, D, QK), shape(D, D), shape(2, R, QK), shape(R, D),
        ),
        in_specs=[any_space] * 12,
        out_specs=(vmem,) * 9,
        scratch_shapes=[
            scratch(2, D, QK), scratch(D, D), scratch(2, R, QK), scratch(R, D),
            scratch(2, R, QK), scratch(R, D), scratch(2, R, QK), scratch(R, D), scratch(2, D), scratch(2, D),
            scratch(512, TILE), scratch(256, TILE), scratch(512, TILE), scratch(256, TILE),
            scratch(2, D, QK), scratch(D, D),
            scratch(2, D, QK, dtype=bf16), scratch(2, D, QK, dtype=bf16), scratch(D, D, dtype=bf16), scratch(D, D, dtype=bf16),
            scratch(4, 256, TILE), scratch(4, 15, 16, TILE), scratch(4, 256, TILE),
            scratch(2, 512, TILE), scratch(2, 15, 32, TILE), scratch(2, 512, TILE),
            scratch(2, 128, TILE), scratch(2, 15, 8, TILE), scratch(2, 128, TILE),
            scratch(2, 8, TILE), scratch(8, TILE), scratch(8, TILE), scratch(15, 8, TILE), scratch(2, 8, TILE),
            scratch(R, D), scratch(2, R, D), scratch(R, D), scratch(2, R, QK),
            scratch(D, 3 * R, dtype=bf16), scratch(2, D, 3 * R, dtype=bf16),
            scratch(8, TILE), scratch(7, 8, TILE),
            pltpu.SemaphoreType.DMA((24,)), pltpu.SemaphoreType.DMA((16,)), pltpu.SemaphoreType.DMA((16,)),
        ],
        compiler_params=pltpu.CompilerParams(collective_id=0, has_side_effects=True, vmem_limit_bytes=48 * 1024 * 1024),
    )(
        pair_grads[0, 0], value_grads[0, 0], pair_errors[0, 0], value_errors[0, 0], pair_basis[0], value_basis[0],
        pair_moment[0], value_moment[0], pair_weights[0], value_weights[0], gain_grads[0, 0], norm_gains[0],
    )
    pparams, vparams, pvel, vvel, gparams, presidue, vresidue, pfactor, vfactor = out
    return (
        pparams[None], vparams[None], pvel[None], vvel[None], gparams[None],
        presidue[None, None], vresidue[None, None], pfactor[None], vfactor[None],
    )


def solution(mesh):
    in_specs = (
        P("dp", "section", None, None, None),
        P("dp", "section", None, None),
        P("dp", "section", None, None, None),
        P("dp", "section", None, None),
        P("section", None, None, None),
        P("section", None, None),
        P("section", None, "dp", None),
        P("section", "dp", None),
        P("section", None, "dp", None),
        P("section", "dp", None),
        P("dp", "section", None, None),
        P("section", None, None),
    )
    out_specs = (
        P("section", None, "dp", None),
        P("section", "dp", None),
        P("section", None, "dp", None),
        P("section", "dp", None),
        P("section", None, None),
        P("dp", "section", None, None, None),
        P("dp", "section", None, None),
        P("section", None, None, None),
        P("section", None, None),
    )
    return jax.shard_map(local, mesh=mesh, in_specs=in_specs, out_specs=out_specs, check_vma=False)
```

time: 580 us -> 77.6 us (0.13)
  waiting for transfers between devices: 342 us -> 0 us
  other arithmetic: 85.7 us -> 0 us
  blocking collectives: 73.3 us -> 0 us
  Pallas kernels: 0 us -> 60.5 us
  matrix products: 55.5 us -> 0 us
  between operations: 16.8 us -> 0.68 us
  local copies, waits for them, and re-layouts: 3.96 us -> 16 us
    psum x4 -> x0, waiting for transfers between devices: 342 us -> none  [the longest x2 198 us: local(): pair_right, value_right = lax.psum((pair_term, value_term), 'dp')]
    psum x2 -> x0, blocking collectives: 73.3 us -> none  [the longest x1 64.3 us: local(): gain_mean = lax.psum(gain_grads[0], 'dp') / replicas]
    another operation x42 -> x0, other arithmetic: 71 us -> none  [the longest x25 38.7 us: whiten(): lower = jnp.linalg.cholesky(gram)]
    pallas_call x0 -> x1, Pallas kernels: none -> 60.5 us  [local(): pl.pallas_call(kernel, name='power_rounds', out_shape=(shape(2, R, QK), s...]
    dot_general x18 -> x0, matrix products: 46.4 us -> none  [the longest x2 11.3 us: local(): jnp.einsum('arn,amn->arm', value_hat, value_full, precision=highest)]
    unnamed x32 -> x29, local copies, waits for them, and re-layouts: 3.37 us -> 16 us
    another operation x8 -> x0, matrix products: 9.08 us -> none  [whiten(): lax.linalg.triangular_solve(lower, factor, left_side=True, lower=True)]
    broadcast_in_dim x2 -> x0, other arithmetic: 6.33 us -> none  [the longest x1 3.91 us: local(): value_residue = (value_full - value_approx)[None]]
  transfers between devices with their start and end apart: 4 -> 0, of which waited for: 4 -> 0; matrix products, arithmetic and copies ran while one was open for 0% -> 0% of each run, Pallas kernels for 0% -> 0%
where the time goes in v1:
time: 77.6 us; the launch traced here: 77.2 us
  Pallas kernels  60.5 us (78%)
  local copies, waits for them, and re-layouts  16 us (21%)
    pallas_call x1, Pallas kernels, local(): pl.pallas_call(kernel, name='power_rounds', out_shape=(shape(2, R, QK), s...  60.5 us
    unnamed x29, local copies, waits for them, and re-layouts  16 us

profile of v1, /device:TPU:1, one launch (start us, length us, event | category | flops | bytes accessed | tf_op | source)
XLA Modules:
  0.0 77.2 jit_solution(17452947383709467111)
XLA Ops:
  0.6 0.0 copy-start
  0.7 1.6 %copy-done = f32[1,1,2,1024,256]{4,3,2,1,0:T(8,128)S(1)} copy-done((f32[1,1,2,1024,256]{4,3,2,1,0:T(8,128)S(1)}, f32[1,1,2,1024,256]{4,3,2,1,0:T(8,128)}, u32[]{:S(2)}) %copy-start) | copy-done | bytes 2097176
  2.2 0.0 copy-start.1
  2.2 0.9 %copy-done.1 = f32[1,32,1024]{2,1,0:T(8,128)S(1)} copy-done((f32[1,32,1024]{2,1,0:T(8,128)S(1)}, f32[1,32,1024]{2,1,0:T(8,128)}, u32[]{:S(2)}) %copy-start.1) | copy-done | bytes 131096
  3.1 0.0 copy-start.2
  3.1 0.9 %copy-done.2 = f32[1,32,1024]{2,1,0:T(8,128)S(1)} copy-done((f32[1,32,1024]{2,1,0:T(8,128)S(1)}, f32[1,32,1024]{2,1,0:T(8,128)}, u32[]{:S(2)}) %copy-start.2) | copy-done | bytes 131096
  4.1 0.9 %copy-done.3 = f32[1,32,1024]{2,1,0:T(8,128)S(1)} copy-done((f32[1,32,1024]{2,1,0:T(8,128)S(1)}, f32[1,32,1024]{2,1,0:T(8,128)}, u32[]{:S(2)}) %copy-start.3) | copy-done | bytes 131096
  5.0 0.8 %copy-done.4 = f32[1,2,32,256]{3,2,1,0:T(8,128)S(1)} copy-done((f32[1,2,32,256]{3,2,1,0:T(8,128)S(1)}, f32[1,2,32,256]{3,2,1,0:T(8,128)}, u32[]{:S(2)}) %copy-start.4) | copy-done | bytes 65560
  5.8 0.8 %copy-done.5 = f32[1,2,32,256]{3,2,1,0:T(8,128)S(1)} copy-done((f32[1,2,32,256]{3,2,1,0:T(8,128)S(1)}, f32[1,2,32,256]{3,2,1,0:T(8,128)}, u32[]{:S(2)}) %copy-start.5) | copy-done | bytes 65560
  6.6 0.8 %copy-done.6 = f32[1,2,32,256]{3,2,1,0:T(8,128)S(1)} copy-done((f32[1,2,32,256]{3,2,1,0:T(8,128)S(1)}, f32[1,2,32,256]{3,2,1,0:T(8,128)}, u32[]{:S(2)}) %copy-start.6) | copy-done | bytes 65560
  7.5 0.7 copy-done.7
  8.2 0.7 copy-done.8
  8.9 60.5 %power_rounds.1 = (f32[2,32,256]{2,1,0:T(8,128)S(1)}, f32[32,1024]{1,0:T(8,128)S(1)}, f32[2,32,256]{2,1,0:T(8,128)S(1)}, f32[32,1024]{1,0:T(8,128)S(1)}, f32[2,1...) custom-call(f32[2,1024,256]{2,1,0:T(8,128)S(1)} %bitcast.21, ...), custom_call_target="tpu_custom_call" | custom-call | tf_op jit(solution)/shard_map/power_rounds/pallas_call | solution.py:431
  69.4 0.0 copy-start.9
  69.4 0.6 copy.30
  70.1 0.7 copy.31
  70.7 0.6 copy.32
  71.4 0.7 copy.33
  72.0 0.6 copy.34
  72.6 1.3 %copy.35 = f32[1,1,2,1024,256]{4,3,2,1,0:T(8,128)} copy(f32[1,1,2,1024,256]{4,3,2,1,0:T(8,128)S(1)} %bitcast.22) | data formatting | bytes 4194304
  73.9 0.0 copy-done.9
  73.9 2.0 %copy.36 = f32[1,1,1024,1024]{3,2,1,0:T(8,128)} copy(f32[1,1,1024,1024]{3,2,1,0:T(8,128)S(1)} %bitcast.40) | data formatting | bytes 8388608
  75.9 0.6 copy.37
  76.6 0.7 copy.38
  (6 shorter events, 0.0 us)
Async XLA Ops:
  0.6 1.6 %copy-start = (f32[1,1,2,1024,256]{4,3,2,1,0:T(8,128)S(1)}, f32[1,1,2,1024,256]{4,3,2,1,0:T(8,128)}, u32[]{:S(2)}) copy-start(f32[1,1,2,1024,256]{4,3,2,1,0:T(8,128)} %param.12) | copy-start | bytes 6291460
  2.2 0.9 %copy-start.1 = (f32[1,32,1024]{2,1,0:T(8,128)S(1)}, f32[1,32,1024]{2,1,0:T(8,128)}, u32[]{:S(2)}) copy-start(f32[1,32,1024]{2,1,0:T(8,128)} %param.17) | copy-start | bytes 393220
  3.1 0.9 %copy-start.2 = (f32[1,32,1024]{2,1,0:T(8,128)S(1)}, f32[1,32,1024]{2,1,0:T(8,128)}, u32[]{:S(2)}) copy-start(f32[1,32,1024]{2,1,0:T(8,128)} %param.19) | copy-start | bytes 393220
  4.0 0.9 %copy-start.3 = (f32[1,32,1024]{2,1,0:T(8,128)S(1)}, f32[1,32,1024]{2,1,0:T(8,128)}, u32[]{:S(2)}) copy-start(f32[1,32,1024]{2,1,0:T(8,128)} %param.21) | copy-start | bytes 393220
  5.0 0.8 %copy-start.4 = (f32[1,2,32,256]{3,2,1,0:T(8,128)S(1)}, f32[1,2,32,256]{3,2,1,0:T(8,128)}, u32[]{:S(2)}) copy-start(f32[1,2,32,256]{3,2,1,0:T(8,128)} %param.16) | copy-start | bytes 196612
  5.8 0.8 %copy-start.5 = (f32[1,2,32,256]{3,2,1,0:T(8,128)S(1)}, f32[1,2,32,256]{3,2,1,0:T(8,128)}, u32[]{:S(2)}) copy-start(f32[1,2,32,256]{3,2,1,0:T(8,128)} %param.18) | copy-start | bytes 196612
  6.6 0.8 %copy-start.6 = (f32[1,2,32,256]{3,2,1,0:T(8,128)S(1)}, f32[1,2,32,256]{3,2,1,0:T(8,128)}, u32[]{:S(2)}) copy-start(f32[1,2,32,256]{3,2,1,0:T(8,128)} %param.20) | copy-start | bytes 196612
  7.5 0.7 copy-start.7
  8.2 0.7 copy-start.8
  69.4 4.5 %copy-start.9 = (f32[1024,1024]{1,0:T(8,128)S(1)}, f32[1024,1024]{1,0:T(8,128)}, u32[]{:S(2)}) copy-start(f32[1024,1024]{1,0:T(8,128)} %get-tuple-element.24) | copy-start | bytes 12582916

commit v2 on v1

--- a/solution.py
+++ b/solution.py
@@ -164,16 +164,16 @@
     for copy in basis_loads:
         copy.wait()
 
-    def pair_stage(out):
-        for w, r, a, b in pair_loads:
+    def pair_stage(out, part=slice(None)):
+        for w, r, a, b in pair_loads[part]:
             a.wait()
             b.wait()
             full = presidue[w, r : r + 512, :] + ep[w, r : r + 512, :]
             presidue[w, r : r + 512, :] = full
             store_tiles(out, w * 8 + r // TILE, product(pb[w], *split(full), NT))
 
-    def value_stage(out):
-        for r, a, b in value_loads:
+    def value_stage(out, part=slice(None)):
+        for r, a, b in value_loads[part]:
             a.wait()
             b.wait()
             full = vresidue[r : r + 256, :] + ev[r : r + 256, :]
@@ -230,6 +230,10 @@
             return [load_tiles(ref, w * right_tiles, right_tiles) for w in range(count)]
 
         def first_wait():
+            if core == 0:
+                put(presidue, p_other, BULK, partner)
+            else:
+                put(vresidue, v_other, BULK, partner)
             state["inverse"] = inverse_factors([gram(b) for b in bases()])
 
         def gains():
@@ -267,8 +271,6 @@
         for step in range(2):
             last = step == 1
             sum_over_plane(2 * step, left_pay[step], left_rs[step], left_res[step], left_rows, state.pop("overlap", first_wait), None if last else chip_sums)
-            if not last:
-                spread_gains()
             left = [whiten(i, a) for i, a in zip(state["inverse"], lefts(left_res[step]))]
             for w, a in enumerate(left):
                 store_tiles(right_pay[step], w * right_tiles, product(a, *mats(w), NN))
@@ -282,6 +284,8 @@
                             lhv[...] = hat
                         else:
                             lhp[w] = hat
+                else:
+                    spread_gains()
 
             def after():
                 if last:
@@ -346,11 +350,11 @@
     @pl.when(c == 0)
     def _():
         pair_stage(pl_pay.at[0])
+        value_stage(v_own, slice(0, 2))
         pl.semaphore_wait(barrier, len(OFFSETS) + len(line))
         put(pl_pay.at[0], p_in, PRODUCT, partner)
         spread_gain(0)
-        value_stage(v_own)
-        put(presidue, p_other, BULK, partner)
+        value_stage(v_own, slice(2, 4))
         arrived(v_in, PRODUCT)
         v_pay[0] = v_own[...] + v_in[...]
         gone(p_in, PRODUCT)
@@ -368,11 +372,11 @@
     @pl.when(c == 1)
     def _():
         value_stage(v_own)
+        pair_stage(p_own, slice(0, 2))
         pl.semaphore_wait(barrier, len(OFFSETS) + len(line))
         put(v_own, v_in, PRODUCT, partner)
         spread_gain(1)
-        pair_stage(p_own)
-        put(vresidue, v_other, BULK, partner)
+        pair_stage(p_own, slice(2, 4))
         arrived(p_in, PRODUCT)
         pl_pay[0] = p_own[...] + p_in[...]
         gone(v_in, PRODUCT)
@@ -390,24 +394,27 @@
 
     for copy in late_loads:
         copy.wait()
+    arrived(g_mean.at[0], GAIN_MEAN)
+    gone(g_mean.at[0], GAIN_MEAN)
+    rows = pl.ds(pl.multiple_of(d * R, R), R)
+    vterm = lax.dot_general(ltv[rows, :], right_stack(rv[...]), NN, preferred_element_type=f32)
+    pterms = [lax.dot_general(ltp[w, rows, :], right_stack(rp[w]), NN, preferred_element_type=f32) for w in range(2)]
+    rv[...] = vterm
+    for w in range(2):
+        rp[w] = pterms[w]
     arrived(totals, TOTAL)
     gone(totals, TOTAL)
-    arrived(g_mean.at[0], GAIN_MEAN)
-    gone(g_mean.at[0], GAIN_MEAN)
     total = part[...]
     for k in range(len(line)):
         total = total + totals[k]
     total = jnp.sum(jnp.sum(total, axis=0, keepdims=True), axis=1, keepdims=True)
     entries = SECTIONS * (2 * D * QK + D * D + 2 * D)
     scale = 1.0 / jnp.sqrt(total / entries + 1e-06)
-    rows = pl.ds(pl.multiple_of(d * R, R), R)
-    term = lax.dot_general(ltv[rows, :], right_stack(rv[...]), NN, preferred_element_type=f32)
-    velocity = momentum_rate * vm[...] + scale * term
+    velocity = momentum_rate * vm[...] + scale * rv[...]
     vvel[...] = velocity
     vparams[...] = vw[...] - step_rate * velocity
     for w in range(2):
-        term = lax.dot_general(ltp[w, rows, :], right_stack(rp[w]), NN, preferred_element_type=f32)
-        velocity = momentum_rate * pm[w] + scale * term
+        velocity = momentum_rate * pm[w] + scale * rp[w]
         pvel[w] = velocity
         pparams[w] = pw[w] - step_rate * velocity
         for t in range(8):
@@ -415,11 +422,21 @@
             gparams[w : w + 1, at] = gn[w : w + 1, at] - step_rate * scale * g_mean[w, t : t + 1, :]
 
 
+def write_out(*refs):
+    count = len(refs) // 2
+    sems = refs[-1]
+    copies = [pltpu.make_async_copy(refs[i], refs[count + i], sems.at[i]) for i in (6, 5, 0, 1, 2, 3, 4, 7, 8)]
+    for copy in copies:
+        copy.start()
+    for copy in copies:
+        copy.wait()
+
+
 def local(
     pair_grads, value_grads, pair_errors, value_errors, pair_basis, value_basis,
     pair_moment, value_moment, pair_weights, value_weights, gain_grads, norm_gains,
 ):
-    any_space = pl.BlockSpec(memory_space=pl.ANY)
+    any_space = pl.BlockSpec(memory_space=pltpu.HBM)
     vmem = pl.BlockSpec(memory_space=pltpu.VMEM)
 
     def shape(*dims):
@@ -452,11 +469,20 @@
             scratch(8, TILE), scratch(7, 8, TILE),
             pltpu.SemaphoreType.DMA((24,)), pltpu.SemaphoreType.DMA((16,)), pltpu.SemaphoreType.DMA((16,)),
         ],
-        compiler_params=pltpu.CompilerParams(collective_id=0, has_side_effects=True, vmem_limit_bytes=48 * 1024 * 1024),
-    )(
+        compiler_params=pltpu.CompilerParams(collective_id=0, has_side_effects=True, vmem_limit_bytes=36 * 1024 * 1024),
+    )(*(pltpu.with_memory_space_constraint(a, pltpu.HBM) for a in (
         pair_grads[0, 0], value_grads[0, 0], pair_errors[0, 0], value_errors[0, 0], pair_basis[0], value_basis[0],
         pair_moment[0], value_moment[0], pair_weights[0], value_weights[0], gain_grads[0, 0], norm_gains[0],
-    )
+    )))
+    out = pl.pallas_call(
+        write_out,
+        name="write_out",
+        out_shape=tuple(jax.ShapeDtypeStruct(a.shape, f32) for a in out),
+        in_specs=[vmem] * 9,
+        out_specs=(pl.BlockSpec(memory_space=pltpu.HBM),) * 9,
+        scratch_shapes=[pltpu.SemaphoreType.DMA((9,))],
+        compiler_params=pltpu.CompilerParams(vmem_limit_bytes=16 * 1024 * 1024),
+    )(*out)
     pparams, vparams, pvel, vvel, gparams, presidue, vresidue, pfactor, vfactor = out
     return (
         pparams[None], vparams[None], pvel[None], vvel[None], gparams[None],

time: 77.6 us -> 62.4 us (0.80)
  local copies, waits for them, and re-layouts: 16 us -> 0 us
  Pallas kernels: 60.5 us -> 61.4 us
    unnamed x29 -> x0, local copies, waits for them, and re-layouts: 16 us -> none
    pallas_call x0 -> x1, Pallas kernels: none -> 2.89 us  [local(): pl.pallas_call(write_out, name='write_out', out_shape=tuple((jax.ShapeDty...]
    pallas_call x1, Pallas kernels: 60.5 us -> 58.6 us  [local(): pl.pallas_call(kernel, name='power_rounds', out_shape=(shape(2, R, QK), s...]
where the time goes in v2:
time: 62.4 us; the launch traced here: 62.3 us
  Pallas kernels  61.4 us (98%)
  between operations  0.82 us (1%)
    pallas_call x1, Pallas kernels, local(): pl.pallas_call(kernel, name='power_rounds', out_shape=(shape(2, R, QK), s...  58.6 us
    pallas_call x1, Pallas kernels, local(): pl.pallas_call(write_out, name='write_out', out_shape=tuple((jax.ShapeDty...  2.89 us

profile of v2, /device:TPU:1, one launch (start us, length us, event | category | flops | bytes accessed | tf_op | source)
XLA Modules:
  0.0 62.3 jit_solution(383217960527842462)
XLA Ops:
  0.6 58.6 %power_rounds.1 = (f32[2,32,256]{2,1,0:T(8,128)S(1)}, f32[32,1024]{1,0:T(8,128)S(1)}, f32[2,32,256]{2,1,0:T(8,128)S(1)}, f32[32,1024]{1,0:T(8,128)S(1)}, f32[2,1...) custom-call(f32[2,1024,256]{2,1,0:T(8,128)} %bitcast.23, ...), custom_call_target="tpu_custom_call" | custom-call | tf_op jit(solution)/shard_map/power_rounds/pallas_call | solution.py:448
  59.2 2.9 %write_out.1 = (f32[2,32,256]{2,1,0:T(8,128)}, f32[32,1024]{1,0:T(8,128)}, f32[2,32,256]{2,1,0:T(8,128)}, f32[32,1024]{1,0:T(8,128)}, f32[2,1024]{1,0:T(2,128)},...) custom-call(f32[2,32,256]{2,1,0:T(8,128)S(1)} %get-tuple-element.27.refs_0_, ...), custom_call_target="tpu_custom_call" | custom-call | tf_op jit(solution)/shard_map/write_out/pallas_call | solution.py:477

commit v3 on v2

--- a/solution.py
+++ b/solution.py
@@ -78,8 +78,9 @@
     pg, vg, pe, ve, pbasis, vbasis, pmoment, vmoment, pweights, vweights, ggrads, gnorm,
     pparams, vparams, pvel, vvel, gparams, presidue, vresidue, pfactor, vfactor,
     ep, ev, pb, vb, pm, vm, pw, vw, gg, gn,
-    p_own, v_own, p_in, v_in, p_other, v_other, ph, plow, vh, vlow,
-    v_pay, v_rs, v_res, pl_pay, pl_rs, pl_res, pr_pay, pr_rs, pr_res,
+    p_own, v_own, p_in, v_in, p_other, v_other, ph, plow, vh, vlow, pth, ptlow, vth, vtlow,
+    v_pay, v_rs, v_res, pl_pay, pl_rs, pl_res,
+    vr_pay, vr_in, vr_mid, vr_next, vr_res, pr_pay, pr_in, pr_mid, pr_next, pr_res,
     g_own, g_pair, g_send, g_in, g_mean,
     lhv, lhp, rv, rp, ltv, ltp, part, totals,
     load, send, recv,
@@ -209,6 +210,32 @@
         gone(rs, slot)
         gone(rest, slot + 1)
 
+    def sum_over_lines(index, pay, first_in, mid, second_in, res, first, second):
+        slot = 2 * index
+        half = mid.shape[1]
+
+        def exchange(source, target, along_x, slot):
+            for k, step in enumerate((2, 1, 3)):
+                for part in range(2):
+                    other = chip_at(0, step) if along_x[part] else chip_at(step, 0)
+                    put(source[part], target.at[part, k], slot, (other * 2 + c, s))
+
+        def combine(own, pieces):
+            return (own + pieces[0]) + (pieces[1] + pieces[2])
+
+        exchange([pay.at[pl.ds(0, half)], pay.at[pl.ds(half, half)]], first_in, (True, False), slot)
+        first()
+        arrived(first_in, slot)
+        for part in range(2):
+            mid[part] = combine(pay[part * half : (part + 1) * half, :], first_in[part])
+        exchange([mid.at[0], mid.at[1]], second_in, (False, True), slot + 1)
+        second()
+        arrived(second_in, slot + 1)
+        for part in range(2):
+            res[part * half : (part + 1) * half, :] = combine(mid[part], second_in[part])
+        gone(first_in, slot)
+        gone(second_in, slot + 1)
+
     def transposed(factor, out):
         high, low = split(factor)
         high, low = high.astype(f32), low.astype(f32)
@@ -218,9 +245,9 @@
         high, low = split(right * (1.0 / N_DP))
         return jnp.concatenate([high, low, high], axis=0)
 
-    def rounds(core, left_bufs, right_bufs, count, right_tiles, bases, mats):
+    def rounds(core, left_bufs, right_bufs, count, right_tiles, bases, mats, turned):
         left_pay, left_rs, left_res, left_rows = left_bufs
-        right_pay, right_rs, right_res, right_rows = right_bufs
+        right_pay, right_in, right_mid, right_next, right_res = right_bufs
         state = {}
 
         def lefts(ref):
@@ -305,12 +332,21 @@
                         transposed(lhv[...], ltv)
                 else:
                     gain_means()
-
-            sum_over_plane(2 * step + 1, right_pay[step], right_rs[step], right_res[step], right_rows, factor_left, after)
+                    for r in range(0, D, 256):
+                        at = slice(r, r + 256)
+                        if core == 0:
+                            vth[:, at] = vh[at, :].T
+                            vtlow[:, at] = vlow[at, :].T
+                        else:
+                            for w in range(2):
+                                pth[w, :, at] = ph[w, at, :].T
+                                ptlow[w, :, at] = plow[w, at, :].T
+
+            sum_over_lines(2 * step + 1, right_pay[step], right_in[step], right_mid[step], right_next[step], right_res[step], factor_left, after)
             right = [whiten(i, a) for i, a in zip(state["inverse"], rights(right_res[step]))]
             if not last:
                 for w, a in enumerate(right):
-                    store_tiles(left_pay[1], w * 8, product(a, *mats(w), NT))
+                    store_tiles(left_pay[1], w * 8, product(a, *turned(w), NN))
 
                 def factor_right():
                     state["inverse"] = inverse_factors([gram(a) for a in right])
@@ -359,8 +395,8 @@
         v_pay[0] = v_own[...] + v_in[...]
         gone(p_in, PRODUCT)
         bufs = [v_pay.at[0], v_pay.at[1]], [v_rs.at[0], v_rs.at[1]], [v_res.at[0], v_res.at[1]], 16
-        more = [v_pay.at[2], v_pay.at[3]], [v_rs.at[2], v_rs.at[3]], [v_res.at[2], v_res.at[3]], 16
-        (right,) = rounds(0, bufs, more, 1, 8, lambda: [vb[...]], lambda w: (vh[...], vlow[...]))
+        more = [[ref.at[i] for i in range(2)] for ref in (vr_pay, vr_in, vr_mid, vr_next, vr_res)]
+        (right,) = rounds(0, bufs, more, 1, 8, lambda: [vb[...]], lambda w: (vh[...], vlow[...]), lambda w: (vth[...], vtlow[...]))
         rv[...] = right
         put(rv, rv, RIGHT, partner)
         send_part(0, [right])
@@ -381,8 +417,8 @@
         pl_pay[0] = p_own[...] + p_in[...]
         gone(v_in, PRODUCT)
         bufs = [pl_pay.at[0], pl_pay.at[1]], [pl_rs.at[0], pl_rs.at[1]], [pl_res.at[0], pl_res.at[1]], 32
-        more = [pr_pay.at[0], pr_pay.at[1]], [pr_rs.at[0], pr_rs.at[1]], [pr_res.at[0], pr_res.at[1]], 8
-        right = rounds(1, bufs, more, 2, 2, lambda: [pb[0], pb[1]], lambda w: (ph[w], plow[w]))
+        more = [[ref.at[i] for i in range(2)] for ref in (pr_pay, pr_in, pr_mid, pr_next, pr_res)]
+        right = rounds(1, bufs, more, 2, 2, lambda: [pb[0], pb[1]], lambda w: (ph[w], plow[w]), lambda w: (pth[w], ptlow[w]))
         for w in range(2):
             rp[w] = right[w]
         put(rp, rp, RIGHT, partner)
@@ -460,9 +496,11 @@
             scratch(512, TILE), scratch(256, TILE), scratch(512, TILE), scratch(256, TILE),
             scratch(2, D, QK), scratch(D, D),
             scratch(2, D, QK, dtype=bf16), scratch(2, D, QK, dtype=bf16), scratch(D, D, dtype=bf16), scratch(D, D, dtype=bf16),
-            scratch(4, 256, TILE), scratch(4, 15, 16, TILE), scratch(4, 256, TILE),
+            scratch(2, QK, D, dtype=bf16), scratch(2, QK, D, dtype=bf16), scratch(D, D, dtype=bf16), scratch(D, D, dtype=bf16),
+            scratch(2, 256, TILE), scratch(2, 15, 16, TILE), scratch(2, 256, TILE),
             scratch(2, 512, TILE), scratch(2, 15, 32, TILE), scratch(2, 512, TILE),
-            scratch(2, 128, TILE), scratch(2, 15, 8, TILE), scratch(2, 128, TILE),
+            scratch(2, 256, TILE), scratch(2, 2, 3, 128, TILE), scratch(2, 2, 128, TILE), scratch(2, 2, 3, 128, TILE), scratch(2, 256, TILE),
+            scratch(2, 128, TILE), scratch(2, 2, 3, 64, TILE), scratch(2, 2, 64, TILE), scratch(2, 2, 3, 64, TILE), scratch(2, 128, TILE),
             scratch(2, 8, TILE), scratch(8, TILE), scratch(8, TILE), scratch(15, 8, TILE), scratch(2, 8, TILE),
             scratch(R, D), scratch(2, R, D), scratch(R, D), scratch(2, R, QK),
             scratch(D, 3 * R, dtype=bf16), scratch(2, D, 3 * R, dtype=bf16),

time: 62.4 us -> 61.7 us (0.989)
    pallas_call x1, Pallas kernels: 58.6 us -> 57.9 us  [local(): pl.pallas_call(kernel, name='power_rounds', out_shape=(shape(2, R, QK), s...]
where the time goes in v3:
time: 61.7 us; the launch traced here: 61.6 us
  Pallas kernels  60.8 us (99%)
  between operations  0.82 us (1%)
    pallas_call x1, Pallas kernels, local(): pl.pallas_call(kernel, name='power_rounds', out_shape=(shape(2, R, QK), s...  57.9 us
    pallas_call x1, Pallas kernels, local(): pl.pallas_call(write_out, name='write_out', out_shape=tuple((jax.ShapeDty...  2.89 us

profile of v3, /device:TPU:1, one launch (start us, length us, event | category | flops | bytes accessed | tf_op | source)
XLA Modules:
  0.0 61.6 jit_solution(836599123387069649)
XLA Ops:
  0.6 57.9 %power_rounds.1 = (f32[2,32,256]{2,1,0:T(8,128)S(1)}, f32[32,1024]{1,0:T(8,128)S(1)}, f32[2,32,256]{2,1,0:T(8,128)S(1)}, f32[32,1024]{1,0:T(8,128)S(1)}, f32[2,1...) custom-call(f32[2,1024,256]{2,1,0:T(8,128)} %bitcast.23, ...), custom_call_target="tpu_custom_call" | custom-call | tf_op jit(solution)/shard_map/power_rounds/pallas_call | solution.py:484
  58.5 2.9 %write_out.1 = (f32[2,32,256]{2,1,0:T(8,128)}, f32[32,1024]{1,0:T(8,128)}, f32[2,32,256]{2,1,0:T(8,128)}, f32[32,1024]{1,0:T(8,128)}, f32[2,1024]{1,0:T(2,128)},...) custom-call(f32[2,32,256]{2,1,0:T(8,128)S(1)} %get-tuple-element.27.refs_0_, ...), custom_call_target="tpu_custom_call" | custom-call | tf_op jit(solution)/shard_map/write_out/pallas_call | solution.py:515

commit v4 on v3

--- a/solution.py
+++ b/solution.py
@@ -34,7 +34,10 @@
 
 
 def whiten(inverse, a):
-    return lax.dot_general(inverse, a, NN, precision=highest, preferred_element_type=f32)
+    wh, wl = split(inverse)
+    ah, al = split(a)
+    left = jnp.concatenate([wh.astype(f32), wl.astype(f32), wh.astype(f32)], axis=1).astype(bf16)
+    return lax.dot_general(left, jnp.concatenate([ah, ah, al], axis=0), NN, preferred_element_type=f32)
 
 
 def inverse_factors(grams):
@@ -87,18 +90,21 @@
 ):
     d = lax.axis_index("dp")
     s = lax.axis_index("section")
-    c = d % 2
-    chip = d // 2
-    z, x = chip // SIDE, chip % SIDE
+    c = lax.rem(d, 2)
+    chip = lax.div(d, 2)
+    z, x = lax.div(chip, SIDE), lax.rem(chip, SIDE)
+    zs = [lax.rem(z + step, SIDE) * SIDE for step in range(SIDE)]
+    xs = [lax.rem(x + step, SIDE) for step in range(SIDE)]
+    chips = {(dz, dx): zs[dz] + xs[dx] for dz in range(SIDE) for dx in range(SIDE)}
 
     def chip_at(dz, dx):
-        return ((z + dz) % SIDE) * SIDE + (x + dx) % SIDE
+        return chips[dz, dx]
 
     partner = (chip * 2 + 1 - c, s)
     line = tuple((dy, dc) for dy in (2, 1, 3, 0) for dc in (0, 1) if dy or dc)
 
     def on_line(dy, dc):
-        return (chip * 2 + (c + dc) % 2, (s + dy) % SECTIONS)
+        return (chip * 2 + lax.rem(c + dc, 2), lax.rem(s + dy, SECTIONS))
 
     loads = []
 
@@ -398,8 +404,8 @@
         more = [[ref.at[i] for i in range(2)] for ref in (vr_pay, vr_in, vr_mid, vr_next, vr_res)]
         (right,) = rounds(0, bufs, more, 1, 8, lambda: [vb[...]], lambda w: (vh[...], vlow[...]), lambda w: (vth[...], vtlow[...]))
         rv[...] = right
+        send_part(0, [right])
         put(rv, rv, RIGHT, partner)
-        send_part(0, [right])
         value_approx()
         arrived(rp, RIGHT)
         pair_approx()
@@ -421,8 +427,8 @@
         right = rounds(1, bufs, more, 2, 2, lambda: [pb[0], pb[1]], lambda w: (ph[w], plow[w]), lambda w: (pth[w], ptlow[w]))
         for w in range(2):
             rp[w] = right[w]
+        send_part(1, right)
         put(rp, rp, RIGHT, partner)
-        send_part(1, right)
         pair_approx()
         arrived(rv, RIGHT)
         value_approx()

time: 61.7 us -> 61.3 us (level)
  no operation moved by 1% of the time
where the time goes in v4:
time: 61.3 us; the launch traced here: 61.2 us
  Pallas kernels  60.4 us (99%)
  between operations  0.82 us (1%)
    pallas_call x1, Pallas kernels, local(): pl.pallas_call(kernel, name='power_rounds', out_shape=(shape(2, R, QK), s...  57.5 us
    pallas_call x1, Pallas kernels, local(): pl.pallas_call(write_out, name='write_out', out_shape=tuple((jax.ShapeDty...  2.89 us

profile of v4, /device:TPU:1, one launch (start us, length us, event | category | flops | bytes accessed | tf_op | source)
XLA Modules:
  0.0 61.2 jit_solution(11607217670148655787)
XLA Ops:
  0.6 57.5 %power_rounds.1 = (f32[2,32,256]{2,1,0:T(8,128)S(1)}, f32[32,1024]{1,0:T(8,128)S(1)}, f32[2,32,256]{2,1,0:T(8,128)S(1)}, f32[32,1024]{1,0:T(8,128)S(1)}, f32[2,1...) custom-call(f32[2,1024,256]{2,1,0:T(8,128)} %bitcast.23, ...), custom_call_target="tpu_custom_call" | custom-call | tf_op jit(solution)/shard_map/power_rounds/pallas_call | solution.py:490
  58.1 2.9 %write_out.1 = (f32[2,32,256]{2,1,0:T(8,128)}, f32[32,1024]{1,0:T(8,128)}, f32[2,32,256]{2,1,0:T(8,128)}, f32[32,1024]{1,0:T(8,128)}, f32[2,1024]{1,0:T(2,128)},...) custom-call(f32[2,32,256]{2,1,0:T(8,128)S(1)} %get-tuple-element.27.refs_0_, ...), custom_call_target="tpu_custom_call" | custom-call | tf_op jit(solution)/shard_map/write_out/pallas_call | solution.py:521
